TPU v7x, 256 devices: a whole 4x4x8 slice. The times are simulated.
256 devices in a mesh: row: 8 (over z_lo, core), col: 32 (over z_hi, y, x).
Axes of the slice: x: 4, y: 4, z: 8 (z_hi: 2, z_lo: 4; z = z_hi * 4 + z_lo), core: 2. Of those that a mesh axis runs over, the one named last changes fastest.
Arguments:
- features: bfloat16 [512, 768], P(('row', 'col')), may hold values from -6 to 13
- projection: bfloat16 [768, 768], replicated, may hold values from -1 to 2
- classifiers: bfloat16 [786432, 768], P(('row', 'col')), may hold values from -2 to 1
- positive_ids: int32 [512, 8], P(('row', 'col')), may hold values from 0 to 786431, as said below
Outputs:
- new_classifiers: bfloat16 [786432, 768], P(('row', 'col'))
- projection_grad: bfloat16 [768, 768], replicated
- features_grad: bfloat16 [512, 768], P(('row', 'col'))
Inputs may be any that keep to these rules, and one draw needn't show every extreme that they name: `positive_ids`: the k-th id of every row lies in [k * 98304, (k + 1) * 98304).
All inputs are finite; a program needn't handle non-finite values.
Results may differ from a plain program's by a relative error of at most 0.0012.
The roundings to bfloat16 on the way count: a program that leaves them out, or rounds other values in their place, can miss the bound.
Values may be sent and summed in bfloat16 or wider, within the bound.
No kernel may reach another device: no remote copies, remote signals or barrier semaphores. Data moves between devices by JAX's collectives and lax.ppermute only.
A program may use at most 192 MiB of HBM per device.

v0:
```python
import jax
import jax.numpy as jnp
from jax import lax
from jax.sharding import Mesh
from jax.sharding import PartitionSpec as P

ROW = ("row_0", "row_1")
COL = ("col_0", "col_1", "col_2")
ROW_COL = ("row_0", "row_1", "col_0", "col_1", "col_2")


learn_rate = 1.0


def laid_out(tiles, dim):
    dims = list(tiles.shape[1:])
    dims[dim] *= tiles.shape[0]
    return jnp.moveaxis(tiles, 0, dim).reshape(dims)


def gather_in_order(value, axes, sequence):
    tiles = value[None]
    for k in sequence:
        tiles = lax.all_gather(tiles, axes[k], axis=0, tiled=True)
    block = [lax.axis_size(axes[k]) for k in reversed(sequence)]
    tiles = tiles.reshape(*block, *value.shape)
    turned = sorted(range(len(sequence)), key=lambda place: sequence[len(sequence) - 1 - place])
    return tiles.transpose(*turned, *range(len(sequence), tiles.ndim)).reshape(-1, *value.shape)


def gathered_by_axis(value, axes, sequence, dim):
    return laid_out(gather_in_order(value, axes, sequence), dim)


def per_device(features, projection, classifiers, positive_ids):
    own = lax.axis_index(ROW) * lax.axis_size(COL) + lax.axis_index(COL)
    lab_dev = classifiers.shape[0]
    rows_dev = features.shape[0]
    total_rows = rows_dev * lax.axis_size(ROW) * lax.axis_size(COL)
    label_ids = own * lab_dev + jnp.arange(lab_dev, dtype=jnp.int32)
    emb = jnp.dot(features, projection, preferred_element_type=jnp.float32).astype(jnp.bfloat16)
    inner = (
        gathered_by_axis(emb, COL, (0, 1, 2), 0),
        gathered_by_axis(positive_ids, COL, (0, 1, 2), 0),
    )
    emb_piece = gathered_by_axis(inner[0], ROW, (0, 1), 0)
    id_piece = gathered_by_axis(inner[1], ROW, (0, 1), 0)
    logits = lax.dot_general(
        emb_piece, classifiers, (((1,), (1,)), ((), ())), preferred_element_type=jnp.float32
    )
    target = jnp.zeros(logits.shape, jnp.float32)
    for k in range(id_piece.shape[1]):
        target = target + (id_piece[:, k][:, None] == label_ids[None, :]).astype(jnp.float32)
    score_grad = ((jax.nn.sigmoid(logits) - target) / total_rows).astype(jnp.bfloat16)
    block = jnp.dot(score_grad, classifiers, preferred_element_type=jnp.float32)
    partial_value = block
    update = lax.dot_general(
        score_grad, emb_piece, (((0,), (0,)), ((), ())), preferred_element_type=jnp.float32
    )
    partial_value, update = (partial_value, update)
    new_classifiers = (classifiers.astype(jnp.float32) - learn_rate * update).astype(jnp.bfloat16)
    emb_grad = lax.psum_scatter(partial_value, ROW_COL, scatter_dimension=0, tiled=True).astype(
        jnp.bfloat16
    )
    local_term = lax.dot_general(
        features, emb_grad, (((0,), (0,)), ((), ())), preferred_element_type=jnp.float32
    )
    projection_grad = lax.psum(local_term, ROW_COL).astype(jnp.bfloat16)
    features_grad = lax.dot_general(
        emb_grad, projection, (((1,), (1,)), ((), ())), preferred_element_type=jnp.float32
    ).astype(jnp.bfloat16)
    return (new_classifiers, projection_grad, features_grad)


def solution(mesh):
    torus = Mesh(mesh.devices.reshape(4, 2, 2, 4, 4), ("row_0", "row_1", "col_0", "col_1", "col_2"))
    placed = (P(ROW_COL, None), P(), P(ROW_COL, None), P(ROW_COL, None))
    return jax.shard_map(
        per_device,
        mesh=torus,
        in_specs=placed,
        out_specs=(P(ROW_COL, None), P(), P(ROW_COL, None)),
        check_vma=False,
    )
```

profile of v0, /device:TPU:1, one launch (start us, length us, event | category | flops | bytes accessed | tf_op | source)
XLA Modules:
  0.0 336.1 jit_solution(3723478858777167202)
XLA Ops:
  0.6 0.0 copy-start
  0.7 9.8 %all-gather.3 = s32[2,2,8]{2,1,0:T(2,128)S(1)} all-gather(s32[1,2,8]{2,1,0:T(2,128)} %bitcast.58), channel_id=3, replica_groups=mesh['row_0'=4,'row_1'=2,'col_0'=2,'col_1'=4,'col_2'=4] {'col_0'}, dimensions={0}, use_global_device_ids=true | all-gather | bytes 192 | tf_op jit(solution)/shard_map/all_gather | solution.py:24
  10.4 8.6 %all_gather.36 = s32[8,2,8]{2,1,0:T(2,128)S(1)} all-gather(s32[2,2,8]{2,1,0:T(2,128)S(1)} %all-gather.3), channel_id=1, replica_groups=mesh['row_0'=4,'row_1'=2,'col_0'=2,'col_1'=4,'col_2'=4] {'col_1'}, dimensions={0}, use_global_device_ids=true | all-gather | bytes 640 | tf_op jit(solution)/shard_map/all_gather | solution.py:24
  19.1 9.6 %all_gather.37 = s32[32,2,8]{2,1,0:T(2,128)S(1)} all-gather(s32[8,2,8]{2,1,0:T(2,128)S(1)} %all_gather.36), channel_id=1, replica_groups=mesh['row_0'=4,'row_1'=2,'col_0'=2,'col_1'=4,'col_2'=4] {'col_2'}, dimensions={0}, use_global_device_ids=true | all-gather | bytes 2560 | tf_op jit(solution)/shard_map/all_gather | solution.py:24
  28.7 0.1 copy.21
  28.8 10.3 %all_gather.38 = s32[4,64,8]{1,2,0:T(8,128)S(1)} all-gather(s32[1,64,8]{1,2,0:T(8,128)S(1)} %copy.21), channel_id=1, replica_groups=mesh['row_0'=4,'row_1'=2,'col_0'=2,'col_1'=4,'col_2'=4] {'row_0'}, dimensions={0}, use_global_device_ids=true | all-gather | bytes 10240 | tf_op jit(solution)/shard_map/all_gather | solution.py:24
  39.1 11.2 %all_gather.39 = s32[8,64,8]{1,2,0:T(8,128)S(1)} all-gather(s32[4,64,8]{1,2,0:T(8,128)S(1)} %all_gather.38), channel_id=1, replica_groups=mesh['row_0'=4,'row_1'=2,'col_0'=2,'col_1'=4,'col_2'=4] {'row_1'}, dimensions={0}, use_global_device_ids=true | all-gather | bytes 24576 | tf_op jit(solution)/shard_map/all_gather | solution.py:24
  50.3 0.1 reshape_reshape.7
  50.5 0.0 copy-done
  50.5 1.0 fusion
  51.4 7.3 %all-gather.2 = bf16[2,2,768]{2,1,0:T(2,128)(2,1)S(1)} all-gather(bf16[1,2,768]{2,1,0:T(2,128)(2,1)S(1)} %fusion), channel_id=2, replica_groups=mesh['row_0'=4,'row_1'=2,'col_0'=2,'col_1'=4,'col_2'=4] {'col_0'}, dimensions={0}, use_global_device_ids=true | all-gather | bytes 9216 | tf_op jit(solution)/shard_map/all_gather | solution.py:24
  58.7 9.1 %all_gather.31 = bf16[8,2,768]{2,1,0:T(2,128)(2,1)S(1)} all-gather(bf16[2,2,768]{2,1,0:T(2,128)(2,1)S(1)} %all-gather.2), channel_id=1, replica_groups=mesh['row_0'=4,'row_1'=2,'col_0'=2,'col_1'=4,'col_2'=4] {'col_1'}, dimensions={0}, use_global_device_ids=true | all-gather | bytes 30720 | tf_op jit(solution)/shard_map/all_gather | solution.py:24
  67.8 9.4 %all_gather.32 = bf16[32,2,768]{2,1,0:T(2,128)(2,1)S(1)} all-gather(bf16[8,2,768]{2,1,0:T(2,128)(2,1)S(1)} %all_gather.31), channel_id=1, replica_groups=mesh['row_0'=4,'row_1'=2,'col_0'=2,'col_1'=4,'col_2'=4] {'col_2'}, dimensions={0}, use_global_device_ids=true | all-gather | bytes 122880 | tf_op jit(solution)/shard_map/all_gather | solution.py:24
  77.3 0.1 copy.26
  77.4 11.4 %all_gather.33 = bf16[4,64,768]{2,1,0:T(8,128)(2,1)S(1)} all-gather(bf16[1,64,768]{2,1,0:T(8,128)(2,1)S(1)} %broadcast_in_dim_reshape_reshape.6), channel_id=1, replica_groups=mesh['row_0'=4,'row_1'=2,'col_0'=2,'col_1'=4,'col_2'=4] {'row_0'}, dimensions={0}, use_global_device_ids=true | all-gather | bytes 491520 | tf_op jit(solution)/shard_map/all_gather | solution.py:24
  88.8 11.7 %all_gather.34 = bf16[8,64,768]{2,1,0:T(8,128)(2,1)S(1)} all-gather(bf16[4,64,768]{2,1,0:T(8,128)(2,1)S(1)} %all_gather.33), channel_id=1, replica_groups=mesh['row_0'=4,'row_1'=2,'col_0'=2,'col_1'=4,'col_2'=4] {'row_1'}, dimensions={0}, use_global_device_ids=true | all-gather | bytes 1179648 | tf_op jit(solution)/shard_map/all_gather | solution.py:24
  100.6 0.0 slice-start
  100.6 0.1 copy.19
  100.6 0.0 copy-start.1
  100.6 0.0 slice-start.1
  100.6 10.0 %multiply_convert_fusion = bf16[512,3072]{1,0:T(8,128)(2,1)S(1)} fusion(bf16[512,768]{1,0:T(8,128)(2,1)S(1)} %bitcast.42, bf16[3072,768]{1,0:T(8,128)(2,1)} %param.6, s32[3072]{0:T(1024)S(1)} %iota_add_fusion, s32[512]{0:T(512)S(1)} %bitcast.51, s32[512]{0:T(512)S(1)} %bitcast.52, s32[512]{0:T(512)S(1)} %bitcast.53, s32[512]{0:T(512)S(1)} %bitcast.54, ...), kind=kOutput, calls=%fused_computation.1 | convolution fusion | flops 2461532160 | bytes 8679424 | tf_op jit(solution)/shard_map/dot_general | solution.py:48
  110.6 0.0 copy-done.1
  110.7 0.0 copy-start.3
  110.7 1.6 copy-done.3
  112.3 0.0 slice-done
  112.3 0.0 slice-done.1
  112.3 0.0 copy-start.2
  112.3 2.6 fusion.2
  114.9 84.5 %all-reduce.3 = bf16[512,768]{1,0:T(8,128)(2,1)} all-reduce(f32[512,768]{1,0:T(8,128)S(1)} %fusion.2), channel_id=4, replica_groups=mesh['row_0'=4,'row_1'=2,'col_0'=2,'col_1'=4,'col_2'=4] {'row_0','row_1'..., use_global_device_ids=true, to_apply=%region_0.0.clone | all-reduce | flops 393216 | bytes 2359296
  199.5 0.0 copy-done.2
  199.5 1.2 convolution_bitcast_fusion
  200.7 122.9 %all-reduce.4 = bf16[768,768]{0,1:T(8,128)(2,1)} all-reduce(f32[768,768]{0,1:T(8,128)S(1)} %convolution_bitcast_fusion), channel_id=1, replica_groups=mesh['row_0'=4,'row_1'=2,'col_0'=2,'col_1'=4,'col_2'=4] {'row_0','row_1'..., use_global_device_ids=true, to_apply=%region_1.0 | all-reduce | flops 589824 | bytes 3538944 | tf_op jit(solution)/shard_map/psum | solution.py:68
  323.6 2.4 copy.23
  326.0 1.7 convolution_convert_fusion
  327.7 8.4 %subtract_convert_fusion = bf16[3072,768]{1,0:T(8,128)(2,1)} fusion(bf16[3072,768]{1,0:T(8,128)(2,1)} %param.6, bf16[512,3072]{1,0:T(8,128)(2,1)} %copy-done.3, bf16[512,768]{1,0:T(8,128)(2,1)} %bitcast.43), kind=kOutput, calls=%fused_computation | convolution fusion | flops 2422996992 | bytes 13369344 | tf_op jit(solution)/shard_map/dot_general | solution.py:57
  (6 shorter events, 0.1 us)
Async XLA Ops:
  0.6 49.8 %copy-start = (bf16[768,768]{1,0:T(8,128)(2,1)S(1)}, bf16[768,768]{1,0:T(8,128)(2,1)}, u32[]{:S(2)}) copy-start(bf16[768,768]{1,0:T(8,128)(2,1)} %param.5) | copy-start | bytes 3538948
  100.6 11.7 %slice-start = ((s8[4718592]{0:T(1024)(128)(4,1)}), s8[4194304]{0:T(1024)(128)(4,1)S(1)}, s32[]{:S(2)}) async-start(s8[4718592]{0:T(1024)(128)(4,1)} %bitcast.59), calls=%async_computation | async-start | bytes 8388608
  100.6 10.0 %copy-start.1 = (bf16[4,2,64,768]{3,2,1,0:T(8,128)(2,1)}, bf16[4,2,64,768]{3,2,1,0:T(8,128)(2,1)S(1)}, u32[]{:S(2)}) copy-start(bf16[4,2,64,768]{3,2,1,0:T(8,128)(2,1)S(1)} %copy.19) | copy-start | bytes 2359300
  100.6 11.7 %slice-start.1 = ((s8[4718592]{0:T(1024)(128)(4,1)}), s8[524288]{0:T(1024)(128)(4,1)S(1)}, s32[]{:S(2)}) async-start(s8[4718592]{0:T(1024)(128)(4,1)} %bitcast.59), calls=%async_computation.1 | async-start | bytes 1048576
  110.7 1.6 copy-start.3
  112.3 87.2 %copy-start.2 = (bf16[2,768]{1,0:T(2,128)(2,1)S(1)}, bf16[2,768]{1,0:T(2,128)(2,1)}, u32[]{:S(2)}) copy-start(bf16[2,768]{1,0:T(2,128)(2,1)} %param.4) | copy-start | bytes 9220
where the time goes:
time: 337 us; the launch traced here: 336 us
  blocking collectives  306 us (91%)
  matrix products  24.9 us (7%)
  local copies, waits for them, and re-layouts  4.41 us (1%)
    psum x1, blocking collectives, per_device(): projection_grad = lax.psum(local_term, ROW_COL).astype(jnp.bfloat16)  123 us
    all_gather x10, blocking collectives, gather_in_order(): tiles = lax.all_gather(tiles, axes[k], axis=0, tiled=True)  98.6 us
    unnamed x1, blocking collectives  84.5 us
    dot_general x1, matrix products, per_device(): lax.dot_general(emb_piece, classifiers, (((1,), (1,)), ((), ())), preferr...  9.99 us
    dot_general x1, matrix products, per_device(): lax.dot_general(score_grad, emb_piece, (((0,), (0,)), ((), ())), preferre...  8.39 us

commit v1 on v0

v1 whole, which is shorter than its diff:
```python
import jax
import jax.numpy as jnp
from jax import lax
from jax.experimental import pallas as pl
from jax.experimental.pallas import tpu as pltpu
from jax.sharding import Mesh
from jax.sharding import PartitionSpec as P

AXES = ("zl", "core", "zh", "y", "x")
PLANE = ("y", "x")
LINE = ("zh", "zl")
CHIPS = PLANE + LINE
CORE = "core"
SWAP = ((0, 1), (1, 0))
LANES = 128
SHIFTS = (12, 6, 0)
LABEL_TILE = 768

learn_rate = 1.0
bf16 = jnp.bfloat16
f32 = jnp.float32


def copies_to(sent, axes):
    return lax.all_to_all(sent, axes, 0, 0, tiled=True)


def matmul(a, b, over):
    return lax.dot_general(a, b, (over, ((), ())), preferred_element_type=f32)


def whole(shape, buffers=None):
    mode = {} if buffers is None else {"pipeline_mode": pl.Buffered(buffers)}
    return pl.BlockSpec(shape, lambda *_: (0,) * len(shape), **mode)


def cost(flops, moved):
    return pl.CostEstimate(flops=flops, bytes_accessed=moved, transcendentals=0)


def params(mib):
    return pltpu.CompilerParams(dimension_semantics=("arbitrary",), vmem_limit_bytes=mib << 20)


def start_kernel(features_ref, ids_ref, w_ref, sent_ref, held_ref, rows_ref, own_ref, sems):
    copies = [
        pltpu.make_async_copy(source, target, sems.at[i])
        for i, (source, target) in enumerate(((features_ref, rows_ref), (ids_ref, own_ref), (w_ref, held_ref)))
    ]
    for copy in copies:
        copy.start()
    copies[1].wait()
    ids = own_ref[...]
    digits = [(ids >> shift) & (255 if j == 0 else 63) for j, shift in enumerate(SHIFTS)]
    spare = jnp.zeros((ids.shape[0], LANES - len(digits) * ids.shape[1]), jnp.int32)
    codes = jnp.concatenate([*digits, spare], axis=1).astype(f32).astype(bf16)
    copies[0].wait()
    packed = jnp.concatenate([rows_ref[...], codes], axis=1)
    sent_ref[...] = jnp.broadcast_to(packed[None], sent_ref.shape)
    copies[2].wait()


def started(features, positive_ids, classifiers, times):
    rows, width = features.shape
    vmem = pl.BlockSpec(memory_space=pltpu.VMEM)
    return pl.pallas_call(
        start_kernel,
        name="start",
        out_shape=[
            jax.ShapeDtypeStruct((times, rows, width + LANES), bf16),
            jax.ShapeDtypeStruct(classifiers.shape, bf16),
        ],
        in_specs=[pl.BlockSpec(memory_space=pltpu.HBM)] * 3,
        out_specs=[vmem, vmem],
        scratch_shapes=[
            pltpu.VMEM(features.shape, features.dtype),
            pltpu.VMEM(positive_ids.shape, positive_ids.dtype),
            pltpu.SemaphoreType.DMA((3,)),
        ],
        compiler_params=pltpu.CompilerParams(vmem_limit_bytes=12 << 20),
        cost_estimate=cost(0, classifiers.size * 4),
    )(*(pltpu.with_memory_space_constraint(a, pltpu.HBM) for a in (features, positive_ids, classifiers)))


def rows_kernel(tiles_ref, rows_ref):
    rows_ref[...] = tiles_ref[...].reshape(rows_ref.shape)


def rows_of(tiles):
    count, each, width = tiles.shape
    return pl.pallas_call(
        rows_kernel,
        name="rows",
        out_shape=jax.ShapeDtypeStruct((count * each, width), tiles.dtype),
        in_specs=[pl.BlockSpec(memory_space=pltpu.VMEM)],
        out_specs=pl.BlockSpec(memory_space=pltpu.VMEM),
        compiler_params=pltpu.CompilerParams(vmem_limit_bytes=8 << 20),
        cost_estimate=cost(0, tiles.size * 4),
    )(tiles)


def sum_kernel(pieces_ref, sent_ref, *own):
    total = pieces_ref[0]
    for i in range(1, pieces_ref.shape[0]):
        total = total + pieces_ref[i]
    total = total.astype(sent_ref.dtype)
    for ref in own:
        ref[...] = total
    for i in range(sent_ref.shape[0]):
        sent_ref[i] = total


def summed(pieces, times, dtype, keep):
    one = pieces.shape[1:]
    outs = [jax.ShapeDtypeStruct((times, *one), dtype)]
    if keep:
        outs.append(jax.ShapeDtypeStruct(one, dtype))
    return pl.pallas_call(
        sum_kernel,
        name="sum_copies",
        out_shape=outs,
        in_specs=[pl.BlockSpec(memory_space=pltpu.VMEM)],
        out_specs=[pl.BlockSpec(memory_space=pltpu.VMEM)] * len(outs),
        compiler_params=pltpu.CompilerParams(vmem_limit_bytes=8 << 20),
        cost_estimate=cost(pieces.size, pieces.size * 4),
    )(pieces)


def update_kernel(ga_ref, gb_ref, ea_ref, eb_ref, w_ref, out_ref):
    change = matmul(ga_ref[...], ea_ref[...], ((0,), (0,))) + matmul(gb_ref[...], eb_ref[...], ((0,), (0,)))
    out_ref[...] = (w_ref[...].astype(f32) - learn_rate * change).astype(bf16)


def updated(grads, embs, classifiers):
    labels, width = classifiers.shape
    count = embs[0].shape[0]
    tile = LABEL_TILE
    grad_spec = pl.BlockSpec((count, tile), lambda t: (0, t))
    row_spec = pl.BlockSpec((tile, width), lambda t: (t, 0))
    return pl.pallas_call(
        update_kernel,
        name="update",
        out_shape=jax.ShapeDtypeStruct(classifiers.shape, bf16),
        grid=(labels // tile,),
        in_specs=[grad_spec, grad_spec, whole((count, width), 1), whole((count, width), 1), row_spec],
        out_specs=row_spec,
        compiler_params=params(60),
        cost_estimate=cost(4 * count * labels * width, labels * width * 4),
    )(*grads, *embs, classifiers)


def per_device(features, projection, classifiers, positive_ids):
    lab_dev, width = classifiers.shape
    rows_dev, positives = positive_ids.shape
    devices = lax.axis_size(AXES)
    total_rows = rows_dev * devices
    own = lax.axis_index(AXES)
    sent, held = started(features, positive_ids, classifiers, lax.axis_size(CHIPS))
    labels = jnp.arange(lab_dev, dtype=jnp.int32)
    lane = jnp.arange(LANES, dtype=jnp.int32)
    weight = jnp.zeros((LANES,), f32)
    for j, shift in enumerate(SHIFTS):
        weight = jnp.where(lane == own // (devices // positives) + j * positives, float(1 << shift), weight)

    base = own * lab_dev
    place = (lax.axis_index(LINE) * rows_dev).astype(jnp.uint32)
    sent, held, weight, base, place = lax.optimization_barrier((sent, held, weight, base, place))
    mine = rows_of(copies_to(sent, CHIPS))
    partner = lax.ppermute(mine, CORE, SWAP)

    def score(rows):
        emb = jnp.dot(rows[:, :width], projection, preferred_element_type=f32).astype(bf16)
        ids = jnp.sum(rows[:, width:].astype(f32) * weight[None, :], axis=1)
        label = ids.astype(jnp.int32) - base
        logits = matmul(emb, held, ((1,), (1,)))
        target = (label[:, None] == labels[None, :]).astype(f32)
        return emb, ((jax.nn.sigmoid(logits) - target) / total_rows).astype(bf16)

    emb_mine, grad_mine = score(mine)
    partner, grad_mine = lax.optimization_barrier((partner, grad_mine))
    emb_partner, grad_partner = score(partner)
    theirs = jnp.dot(grad_partner, held, preferred_element_type=f32)
    got = lax.ppermute(theirs, CORE, SWAP)
    ours = jnp.dot(grad_mine, held, preferred_element_type=f32)
    ours, got = lax.optimization_barrier((ours, got))
    ours = ours + got
    plane = lax.axis_size(PLANE)
    line = lax.axis_size(LINE)
    pieces = copies_to(ours.reshape(plane, -1, width), PLANE)
    (sent,) = summed(pieces, line, f32, False)
    sent, line_grad = summed(copies_to(sent, LINE), plane, bf16, True)
    sent, grad_mine, grad_partner = lax.optimization_barrier((sent, grad_mine, grad_partner))
    new_classifiers = updated((grad_mine, grad_partner), (emb_mine, emb_partner), classifiers)
    core_grads = copies_to(sent, PLANE).reshape(-1, width)
    core_grads, new_classifiers = lax.optimization_barrier((core_grads, new_classifiers))
    line_grad, core_grads = lax.optimization_barrier((line_grad, core_grads))
    emb_grad = lax.dynamic_slice(line_grad, (place, jnp.uint32(0)), (rows_dev, width))
    features_grad = matmul(emb_grad, projection, ((1,), (1,))).astype(bf16)
    partner_grads = lax.ppermute(core_grads, CORE, SWAP)
    first = matmul(mine[:, :width], core_grads, ((0,), (0,)))
    first, partner_grads, features_grad = lax.optimization_barrier((first, partner_grads, features_grad))
    projection_grad = (first + matmul(partner[:, :width], partner_grads, ((0,), (0,)))).astype(bf16)
    return new_classifiers, projection_grad, features_grad


def solution(mesh):
    torus = Mesh(mesh.devices.reshape(4, 2, 2, 4, 4), AXES)
    placed = (P(AXES, None), P(), P(AXES, None), P(AXES, None))
    return jax.shard_map(
        per_device,
        mesh=torus,
        in_specs=placed,
        out_specs=(P(AXES, None), P(), P(AXES, None)),
        check_vma=False,
    )
```

time: 337 us -> 100 us (0.30)
  blocking collectives: 306 us -> 66.5 us
  matrix products: 24.9 us -> 9.03 us
  Pallas kernels: 0 us -> 11.1 us
  starting transfers between devices: 0 us -> 9.24 us
  local copies, waits for them, and re-layouts: 4.41 us -> 0.25 us
    psum x1 -> x0, blocking collectives: 123 us -> none  [per_device(): projection_grad = lax.psum(local_term, ROW_COL).astype(jnp.bfloat16)]
    all_gather x10 -> x0, blocking collectives: 98.6 us -> none  [gather_in_order(): tiles = lax.all_gather(tiles, axes[k], axis=0, tiled=True)]
    unnamed x1 -> x0, blocking collectives: 84.5 us -> none
    all_to_all x0 -> x3, blocking collectives: none -> 66.5 us  [copies_to(): return lax.all_to_all(sent, axes, 0, 0, tiled=True)]
    dot_general x6 -> x9, matrix products: 24.9 us -> 9.03 us  [the longest x5 5.28 us: matmul(): return lax.dot_general(a, b, (over, ((), ())), preferred_element_type=f32)]
    pallas_call x0 -> x5, Pallas kernels: none -> 11.1 us  [the longest x1 7.7 us: updated(): pl.pallas_call(update_kernel, name='update', out_shape=jax.ShapeDtypeStru...]
    ppermute x0 -> x3, starting transfers between devices: none -> 5.69 us  [the longest x1 3.05 us: per_device(): partner_grads = lax.ppermute(core_grads, CORE, SWAP)]
    unnamed x13 -> x14, local copies, waits for them, and re-layouts: 4.04 us -> 0.25 us
  transfers between devices with their start and end apart: 0 -> 4, of which waited for: 0 -> 2; matrix products, arithmetic and copies ran while one was open for 0% -> 5% of each run, Pallas kernels for 0% -> 8%
where the time goes in v1:
time: 100 us
  blocking collectives  66.5 us (66%)
  Pallas kernels  11.1 us (11%)
  starting transfers between devices  9.24 us (9%)
  matrix products  9.03 us (9%)
  waiting for transfers between devices  1.59 us (2%)
  other arithmetic  1.56 us (2%)
    all_to_all x3, blocking collectives, copies_to(): return lax.all_to_all(sent, axes, 0, 0, tiled=True)  66.5 us
    pallas_call x1, Pallas kernels, updated(): pl.pallas_call(update_kernel, name='update', out_shape=jax.ShapeDtypeStru...  7.7 us
    dot_general x5, matrix products, matmul(): return lax.dot_general(a, b, (over, ((), ())), preferred_element_type=f32)  5.28 us
    all_to_all x1, starting transfers between devices, copies_to(): return lax.all_to_all(sent, axes, 0, 0, tiled=True)  3.55 us
    ppermute x1, starting transfers between devices, per_device(): partner_grads = lax.ppermute(core_grads, CORE, SWAP)  3.05 us
    ppermute x1, starting transfers between devices, per_device(): partner = lax.ppermute(mine, CORE, SWAP)  2.54 us
    pallas_call x1, Pallas kernels, started(): pl.pallas_call(start_kernel, name='start', out_shape=[jax.ShapeDtypeStruc...  2.49 us
  transfers between devices with their start and end apart: 4, of which 2 were waited for; matrix products, arithmetic and copies ran while one was open for 5% of the time, Pallas kernels for 8%

profile of v1, /device:TPU:1, one launch (start us, length us, event | category | flops | bytes accessed | tf_op | source)
XLA Modules:
  0.0 100.2 jit_solution(16915644351668605971)
XLA Ops:
  0.6 0.0 copy-start
  0.7 2.5 %start.1 = (bf16[128,2,896]{2,1,0:T(2,128)(2,1)S(1)}, bf16[3072,768]{1,0:T(8,128)(2,1)S(1)}) custom-call(bf16[2,768]{1,0:T(2,128)(2,1)} %features_ref.1, s32[2,8]{1,0:T(2,128)} %ids_ref.1, bf16[3072,768]{1,0:T(8,128)(2,1)} %w_ref.3), custom_call_target="tpu_custom_call" | custom-call | bytes 9437184 | tf_op jit(solution)/shard_map/start/pallas_call | solution.py:66
  3.2 33.9 %all_to_all.20.tiles_ref = bf16[128,2,896]{2,1,0:T(2,128)(2,1)S(1)} all-to-all(bf16[128,2,896]{2,1,0:T(2,128)(2,1)S(1)} %get-tuple-element.28), channel_id=1, replica_groups=mesh['zl'=4,'core'=2,'zh'=2,'y'=4,'x'=4] {'y','x','zh','zl'}, dimensions={0} | all-to-all | bytes 917504 | tf_op jit(solution)/shard_map/all_to_all | solution.py:25
  37.1 0.1 rows.1
  37.2 2.5 %collective-permute-start = (bf16[256,896]{1,0:T(8,128)(2,1)S(1)}, bf16[256,896]{1,0:T(8,128)(2,1)S(1)}, u32[]{:S(2)}, u32[]{:S(2)}) collective-permute-start(bf16[256,896]{1,0:T(8,128)(2,1)S(1)} %rows.1), channel_id=1, source_target_pairs={{0,32},{32,0},{1,33},{33,1},{2,34},{34,2},{3,35},{35,3},{4,36},{36... | collective-permute-start | bytes 1376264 | tf_op jit(solution)/shard_map/ppermute | solution.py:169
  39.7 0.1 multiply_reduce_fusion.1
  39.8 0.0 copy-done
  39.8 0.5 convolution_convert_fusion.1.ea_ref
  40.3 0.0 copy-start.5
  40.3 1.6 %fusion.11.ga_ref = bf16[256,3072]{1,0:T(8,128)(2,1)S(1)} fusion(bf16[256,768]{1,0:T(8,128)(2,1)S(1)} %convolution_convert_fusion.1.ea_ref, bf16[3072,768]{1,0:T(8,128)(2,1)S(1)} %get-tuple-element.29, s32[256]{0:T(256)S(1)} %convert_subtract_fusion.1), kind=kOutput, calls=%fused_computation.13 | convolution fusion | flops 1214251008 | bytes 6685696 | tf_op jit(solution)/shard_map/dot_general | solution.py:29
  42.0 0.0 copy-done.5
  42.0 0.0 copy-start.1
  42.0 0.0 collective-permute-done
  42.0 0.0 copy-start.3
  42.0 0.1 multiply_reduce_fusion
  42.1 0.5 convolution_convert_fusion.eb_ref
  42.6 0.2 copy-done.3
  42.8 0.0 copy-start.6
  42.8 1.6 %fusion.7.gb_ref = bf16[256,3072]{1,0:T(8,128)(2,1)S(1)} fusion(bf16[256,768]{1,0:T(8,128)(2,1)S(1)} %convolution_convert_fusion.eb_ref, bf16[3072,768]{1,0:T(8,128)(2,1)S(1)} %get-tuple-element.29, s32[256]{0:T(256)S(1)} %convert_subtract_fusion), kind=kOutput, calls=%fused_computation.9 | convolution fusion | flops 1214251008 | bytes 6685696 | tf_op jit(solution)/shard_map/dot_general | solution.py:29
  44.4 0.0 copy-done.6
  44.5 0.0 copy-start.2
  44.5 1.4 %fusion.21 = f32[256,768]{1,0:T(8,128)S(1)} fusion(bf16[256,3072]{1,0:T(8,128)(2,1)S(1)} %fusion.7.gb_ref, bf16[3072,768]{1,0:T(8,128)(2,1)S(1)} %get-tuple-element.29), kind=kOutput, calls=%fused_computation.36 | convolution fusion | flops 1207959552 | bytes 7077888 | tf_op jit(solution)/shard_map/dot_general | solution.py:182
  45.9 0.0 copy-done.2
  45.9 0.1 collective-permute-start.1
  46.0 0.0 copy-done.1
  46.0 1.4 %fusion.20 = f32[256,768]{1,0:T(8,128)S(1)} fusion(bf16[256,3072]{1,0:T(8,128)(2,1)S(1)} %fusion.11.ga_ref, bf16[3072,768]{1,0:T(8,128)(2,1)S(1)} %get-tuple-element.29), kind=kOutput, calls=%fused_computation.35 | convolution fusion | flops 1207959552 | bytes 7077888 | tf_op jit(solution)/shard_map/dot_general | solution.py:184
  47.4 0.9 collective-permute-done.1
  48.2 0.1 add.43
  48.3 16.7 %all_to_all.21.pieces_ref = f32[16,16,768]{2,1,0:T(8,128)S(1)} all-to-all(f32[16,16,768]{2,1,0:T(8,128)S(1)} %bitcast.15), channel_id=1, replica_groups=mesh['zl'=4,'core'=2,'zh'=2,'y'=4,'x'=4] {'y','x'}, dimensions={0} | all-to-all | bytes 1572864 | tf_op jit(solution)/shard_map/all_to_all | solution.py:25
  65.1 15.9 %all_to_all.22.pieces_ref = f32[8,16,768]{2,1,0:T(8,128)S(1)} all-to-all(f32[8,16,768]{2,1,0:T(8,128)S(1)} %sum_copies.2), channel_id=1, replica_groups=mesh['zl'=4,'core'=2,'zh'=2,'y'=4,'x'=4] {'zh','zl'}, dimensions={0} | all-to-all | bytes 786432 | tf_op jit(solution)/shard_map/all_to_all | solution.py:25
  81.0 0.8 sum_copies.3
  81.8 3.6 %all-to-all-start.3 = ((bf16[16,16,768]{2,1,0:T(8,128)(2,1)}), bf16[16,16,768]{2,1,0:T(8,128)(2,1)S(1)}, u32[]{:S(2)}, u32[]{:S(2)}) async-start(bf16[16,16,768]{2,1,0:T(8,128)(2,1)} %get-tuple-element.37), calls=%async_computation.3 | async-start | bytes 786432 | tf_op jit(solution)/shard_map/all_to_all | solution.py:25
  85.4 7.7 %update.1 = bf16[3072,768]{1,0:T(8,128)(2,1)} custom-call(bf16[256,3072]{1,0:T(8,128)(2,1)} %copy-done.1, bf16[256,3072]{1,0:T(8,128)(2,1)} %copy-done.2, bf16[256,768]{1,0:T(8,128)(2,1)} %copy-done.5, bf16[256,768]{1,0:T(8,128)(2,1)} %copy-done.6, bf16[3072,768]{1,0:T(8,128)(2,1)} %w_ref.3), custom_call_target="tpu_custom_call" | custom-call | flops 2415919104 | bytes 9437184 | tf_op jit(solution)/shard_map/update/pallas_call | solution.py:140
  93.1 0.0 copy-start.4
  93.1 0.7 all-to-all-done.3
  93.8 3.1 %collective-permute-start.2 = (bf16[256,768]{1,0:T(8,128)(2,1)S(1)}, bf16[256,768]{1,0:T(8,128)(2,1)S(1)}, u32[]{:S(2)}, u32[]{:S(2)}) collective-permute-start(bf16[256,768]{1,0:T(8,128)(2,1)S(1)} %bitcast.16), channel_id=1, source_target_pairs={{0,32},{32,0},{1,33},{33,1},{2,34},{34,2},{3,35},{35,3},{4,36},{36... | collective-permute-start | bytes 1179656 | tf_op jit(solution)/shard_map/ppermute | solution.py:199
  96.9 1.0 %convolution_convert_fusion.2 = bf16[2,768]{1,0:T(2,128)(2,1)} fusion(bf16[768,768]{1,0:T(8,128)(2,1)S(1)} %copy-done, bf16[16,768]{1,0:T(8,128)(2,1)S(1)} %get-tuple-element.44, u32[]{:T(128)S(6)} %convert_element_type.47), kind=kOutput, calls=%fused_computation.19 | convolution fusion | flops 2360832 | bytes 1185796 | tf_op jit(solution)/shard_map/dot_general | solution.py:29
  97.9 0.5 fusion.12
  98.4 0.0 collective-permute-done.2
  98.4 0.0 copy-done.4
  98.4 0.5 fusion.15
  98.9 1.2 %add_convert_fusion = bf16[768,768]{1,0:T(8,128)(2,1)} fusion(f32[768,768]{1,0:T(8,128)S(1)} %fusion.12, f32[768,768]{1,0:T(8,128)S(1)} %fusion.15), kind=kLoop, calls=%fused_computation.16 | loop fusion | flops 1179648 | bytes 5898240 | tf_op jit(solution)/shard_map/convert_element_type | solution.py:202
  (4 shorter events, 0.1 us)
Async XLA Ops:
  0.6 39.2 %copy-start = (bf16[768,768]{1,0:T(8,128)(2,1)S(1)}, bf16[768,768]{1,0:T(8,128)(2,1)}, u32[]{:S(2)}) copy-start(bf16[768,768]{1,0:T(8,128)(2,1)} %param.5) | copy-start | bytes 3538948
  37.2 4.8 %collective-permute-start = (bf16[256,896]{1,0:T(8,128)(2,1)S(1)}, bf16[256,896]{1,0:T(8,128)(2,1)S(1)}, u32[]{:S(2)}, u32[]{:S(2)}) collective-permute-start(bf16[256,896]{1,0:T(8,128)(2,1)S(1)} %rows.1), channel_id=1, source_target_pairs={{0,32},{32,0},{1,33},{33,1},{2,34},{34,2},{3,35},{35,3},{4,36},{36... | collective-permute-start | bytes 1376264 | tf_op jit(solution)/shard_map/ppermute | solution.py:169
  40.3 1.6 %copy-start.5 = (bf16[256,768]{1,0:T(8,128)(2,1)}, bf16[256,768]{1,0:T(8,128)(2,1)S(1)}, u32[]{:S(2)}) copy-start(bf16[256,768]{1,0:T(8,128)(2,1)S(1)} %convolution_convert_fusion.1.ea_ref) | copy-start | bytes 1179652
  42.0 4.0 %copy-start.1 = (bf16[256,3072]{1,0:T(8,128)(2,1)}, bf16[256,3072]{1,0:T(8,128)(2,1)S(1)}, u32[]{:S(2)}) copy-start(bf16[256,3072]{1,0:T(8,128)(2,1)S(1)} %fusion.11.ga_ref) | copy-start | bytes 4718596
  42.0 0.8 copy-start.3
  42.8 1.6 %copy-start.6 = (bf16[256,768]{1,0:T(8,128)(2,1)}, bf16[256,768]{1,0:T(8,128)(2,1)S(1)}, u32[]{:S(2)}) copy-start(bf16[256,768]{1,0:T(8,128)(2,1)S(1)} %convolution_convert_fusion.eb_ref) | copy-start | bytes 1179652
  44.5 1.4 %copy-start.2 = (bf16[256,3072]{1,0:T(8,128)(2,1)}, bf16[256,3072]{1,0:T(8,128)(2,1)S(1)}, u32[]{:S(2)}) copy-start(bf16[256,3072]{1,0:T(8,128)(2,1)S(1)} %fusion.7.gb_ref) | copy-start | bytes 4718596
  45.9 2.4 %collective-permute-start.1 = (f32[256,768]{1,0:T(8,128)S(1)}, f32[256,768]{1,0:T(8,128)S(1)}, u32[]{:S(2)}, u32[]{:S(2)}) collective-permute-start(f32[256,768]{1,0:T(8,128)S(1)} %fusion.21), channel_id=1, source_target_pairs={{0,32},{32,0},{1,33},{33,1},{2,34},{34,2},{3,35},{35,3},{4,36},{36... | collective-permute-start | bytes 2359304 | tf_op jit(solution)/shard_map/ppermute | solution.py:183
  81.8 12.0 %all-to-all-start.3 = ((bf16[16,16,768]{2,1,0:T(8,128)(2,1)}), bf16[16,16,768]{2,1,0:T(8,128)(2,1)S(1)}, u32[]{:S(2)}, u32[]{:S(2)}) async-start(bf16[16,16,768]{2,1,0:T(8,128)(2,1)} %get-tuple-element.37), calls=%async_computation.3 | async-start | bytes 786432 | tf_op jit(solution)/shard_map/all_to_all | solution.py:25
  93.1 5.3 %copy-start.4 = (bf16[256,896]{1,0:T(8,128)(2,1)S(1)}, bf16[256,896]{1,0:T(8,128)(2,1)}, u32[]{:S(2)}) copy-start(bf16[256,896]{1,0:T(8,128)(2,1)} %copy-done.3) | copy-start | bytes 1376260
  93.8 4.6 %collective-permute-start.2 = (bf16[256,768]{1,0:T(8,128)(2,1)S(1)}, bf16[256,768]{1,0:T(8,128)(2,1)S(1)}, u32[]{:S(2)}, u32[]{:S(2)}) collective-permute-start(bf16[256,768]{1,0:T(8,128)(2,1)S(1)} %bitcast.16), channel_id=1, source_target_pairs={{0,32},{32,0},{1,33},{33,1},{2,34},{34,2},{3,35},{35,3},{4,36},{36... | collective-permute-start | bytes 1179656 | tf_op jit(solution)/shard_map/ppermute | solution.py:199

commit v2 on v1

--- a/solution.py
+++ b/solution.py
@@ -14,7 +14,7 @@
 SWAP = ((0, 1), (1, 0))
 LANES = 128
 SHIFTS = (12, 6, 0)
-LABEL_TILE = 768
+UPDATE_TILE = 768
 
 learn_rate = 1.0
 bf16 = jnp.bfloat16
@@ -60,7 +60,7 @@
     copies[2].wait()
 
 
-def started(features, positive_ids, classifiers, times):
+def started(features, positive_ids, projection, times):
     rows, width = features.shape
     vmem = pl.BlockSpec(memory_space=pltpu.VMEM)
     return pl.pallas_call(
@@ -68,7 +68,7 @@
         name="start",
         out_shape=[
             jax.ShapeDtypeStruct((times, rows, width + LANES), bf16),
-            jax.ShapeDtypeStruct(classifiers.shape, bf16),
+            jax.ShapeDtypeStruct(projection.shape, bf16),
         ],
         in_specs=[pl.BlockSpec(memory_space=pltpu.HBM)] * 3,
         out_specs=[vmem, vmem],
@@ -78,8 +78,8 @@
             pltpu.SemaphoreType.DMA((3,)),
         ],
         compiler_params=pltpu.CompilerParams(vmem_limit_bytes=12 << 20),
-        cost_estimate=cost(0, classifiers.size * 4),
-    )(*(pltpu.with_memory_space_constraint(a, pltpu.HBM) for a in (features, positive_ids, classifiers)))
+        cost_estimate=cost(0, projection.size * 4),
+    )(*(pltpu.with_memory_space_constraint(a, pltpu.HBM) for a in (features, positive_ids, projection)))
 
 
 def rows_kernel(tiles_ref, rows_ref):
@@ -126,27 +126,83 @@
     )(pieces)
 
 
-def update_kernel(ga_ref, gb_ref, ea_ref, eb_ref, w_ref, out_ref):
-    change = matmul(ga_ref[...], ea_ref[...], ((0,), (0,))) + matmul(gb_ref[...], eb_ref[...], ((0,), (0,)))
-    out_ref[...] = (w_ref[...].astype(f32) - learn_rate * change).astype(bf16)
-
-
-def updated(grads, embs, classifiers):
-    labels, width = classifiers.shape
+def line_kernel(shifts, at_ref, own_ref, *refs):
+    moved, out_ref = refs[:-1], refs[-1]
+    count = len(shifts) + 1
+    total = None
+    for source in range(count):
+        back = lax.rem(at_ref[0] - source + count, count)
+        value = own_ref[...]
+        for shift, ref in zip(shifts, moved):
+            value = jnp.where(back == shift, ref[...], value)
+        total = value if total is None else total + value
+    out_ref[...] = total
+
+
+def line_summed(at, own, moved, shifts):
+    vmem = pl.BlockSpec(memory_space=pltpu.VMEM)
+
+    def body(*refs):
+        line_kernel(shifts, *refs)
+
+    return pl.pallas_call(
+        body,
+        name="line_sum",
+        out_shape=jax.ShapeDtypeStruct(own.shape, own.dtype),
+        in_specs=[pl.BlockSpec(memory_space=pltpu.SMEM)] + [vmem] * (1 + len(moved)),
+        out_specs=vmem,
+        compiler_params=pltpu.CompilerParams(vmem_limit_bytes=8 << 20),
+        cost_estimate=cost(own.size * 4, own.size * 20),
+    )(at, own, *moved)
+
+
+def pair_kernel(near_ref, far_ref, sent_ref, own_ref):
+    total = (near_ref[...] + far_ref[...]).astype(bf16)
+    own_ref[...] = total
+    for i in range(sent_ref.shape[0]):
+        sent_ref[i] = total
+
+
+def paired(near, far, times):
+    vmem = pl.BlockSpec(memory_space=pltpu.VMEM)
+    return pl.pallas_call(
+        pair_kernel,
+        name="pair_copies",
+        out_shape=[jax.ShapeDtypeStruct((times, *near.shape), bf16), jax.ShapeDtypeStruct(near.shape, bf16)],
+        in_specs=[vmem, vmem],
+        out_specs=[vmem, vmem],
+        compiler_params=pltpu.CompilerParams(vmem_limit_bytes=8 << 20),
+        cost_estimate=cost(near.size, near.size * 8),
+    )(near, far)
+
+
+def update_kernel(ga_ref, gb_ref, ea_ref, eb_ref, w_ref, out_ref, fresh_ref, sems):
+    tile = UPDATE_TILE
+    copies = []
+    for i in range(w_ref.shape[0] // tile):
+        cut = slice(i * tile, (i + 1) * tile)
+        change = matmul(ga_ref[:, cut], ea_ref[...], ((0,), (0,))) + matmul(gb_ref[:, cut], eb_ref[...], ((0,), (0,)))
+        fresh_ref[cut, :] = (w_ref[cut, :].astype(f32) - learn_rate * change).astype(bf16)
+        there = pl.ds(i * tile, tile)
+        copies.append(pltpu.make_async_copy(fresh_ref.at[there], out_ref.at[there], sems.at[i]))
+        copies[-1].start()
+    for copy in copies:
+        copy.wait()
+
+
+def updated(grads, embs, held):
+    labels, width = held.shape
     count = embs[0].shape[0]
-    tile = LABEL_TILE
-    grad_spec = pl.BlockSpec((count, tile), lambda t: (0, t))
-    row_spec = pl.BlockSpec((tile, width), lambda t: (t, 0))
     return pl.pallas_call(
         update_kernel,
         name="update",
-        out_shape=jax.ShapeDtypeStruct(classifiers.shape, bf16),
-        grid=(labels // tile,),
-        in_specs=[grad_spec, grad_spec, whole((count, width), 1), whole((count, width), 1), row_spec],
-        out_specs=row_spec,
-        compiler_params=params(60),
-        cost_estimate=cost(4 * count * labels * width, labels * width * 4),
-    )(*grads, *embs, classifiers)
+        out_shape=jax.ShapeDtypeStruct(held.shape, bf16),
+        in_specs=[pl.BlockSpec(memory_space=pltpu.VMEM)] * 5,
+        out_specs=pl.BlockSpec(memory_space=pltpu.HBM),
+        scratch_shapes=[pltpu.VMEM(held.shape, bf16), pltpu.SemaphoreType.DMA((labels // UPDATE_TILE,))],
+        compiler_params=pltpu.CompilerParams(vmem_limit_bytes=16 << 20),
+        cost_estimate=cost(4 * count * labels * width, labels * width * 2),
+    )(*grads, *embs, held)
 
 
 def per_device(features, projection, classifiers, positive_ids):
@@ -155,7 +211,8 @@
     devices = lax.axis_size(AXES)
     total_rows = rows_dev * devices
     own = lax.axis_index(AXES)
-    sent, held = started(features, positive_ids, classifiers, lax.axis_size(CHIPS))
+    sent, projection = started(features, positive_ids, projection, lax.axis_size(CHIPS))
+    held = classifiers
     labels = jnp.arange(lab_dev, dtype=jnp.int32)
     lane = jnp.arange(LANES, dtype=jnp.int32)
     weight = jnp.zeros((LANES,), f32)
@@ -164,7 +221,8 @@
 
     base = own * lab_dev
     place = (lax.axis_index(LINE) * rows_dev).astype(jnp.uint32)
-    sent, held, weight, base, place = lax.optimization_barrier((sent, held, weight, base, place))
+    at_z = lax.axis_index("zl").reshape(1)
+    sent, projection, weight, base, place, at_z = lax.optimization_barrier((sent, projection, weight, base, place, at_z))
     mine = rows_of(copies_to(sent, CHIPS))
     partner = lax.ppermute(mine, CORE, SWAP)
 
@@ -185,14 +243,19 @@
     ours, got = lax.optimization_barrier((ours, got))
     ours = ours + got
     plane = lax.axis_size(PLANE)
-    line = lax.axis_size(LINE)
     pieces = copies_to(ours.reshape(plane, -1, width), PLANE)
-    (sent,) = summed(pieces, line, f32, False)
-    sent, line_grad = summed(copies_to(sent, LINE), plane, bf16, True)
-    sent, grad_mine, grad_partner = lax.optimization_barrier((sent, grad_mine, grad_partner))
-    new_classifiers = updated((grad_mine, grad_partner), (emb_mine, emb_partner), classifiers)
+    (near,) = summed(pieces, 1, f32, False)
+    near = near[0]
+    count = lax.axis_size("zl")
+    shifts = (2, 1, 3)
+    moved = [lax.ppermute(near, "zl", tuple((i, (i + k) % count) for i in range(count))) for k in shifts]
+    near, grad_mine, grad_partner = lax.optimization_barrier((near, grad_mine, grad_partner))
+    new_classifiers = updated((grad_mine, grad_partner), (emb_mine, emb_partner), held)
+    near, new_classifiers, *moved = lax.optimization_barrier((near, new_classifiers, *moved))
+    near = line_summed(at_z, near, moved, shifts)
+    far = lax.ppermute(near, "zh", SWAP)
+    sent, line_grad = paired(near, far, plane)
     core_grads = copies_to(sent, PLANE).reshape(-1, width)
-    core_grads, new_classifiers = lax.optimization_barrier((core_grads, new_classifiers))
     line_grad, core_grads = lax.optimization_barrier((line_grad, core_grads))
     emb_grad = lax.dynamic_slice(line_grad, (place, jnp.uint32(0)), (rows_dev, width))
     features_grad = matmul(emb_grad, projection, ((1,), (1,))).astype(bf16)

time: 100 us -> 97.3 us (0.973)
  Pallas kernels: 11.1 us -> 5.46 us
  blocking collectives: 66.5 us -> 62.2 us
  starting transfers between devices: 9.24 us -> 12.9 us
  waiting for transfers between devices: 1.59 us -> 5.08 us
    ppermute x0 -> x4, starting transfers between devices: none -> 6.18 us  [the longest x3 3.44 us: per_device(): lax.ppermute(near, 'zl', tuple(((i, (i + k) % count) for i in range(count...]
    all_to_all x3, blocking collectives: 66.5 us -> 62.2 us  [copies_to(): return lax.all_to_all(sent, axes, 0, 0, tiled=True)]
    ppermute x0 -> x4, waiting for transfers between devices: none -> 4.2 us  [the longest x1 4.19 us: per_device(): far = lax.ppermute(near, 'zh', SWAP)]
    pallas_call x1, Pallas kernels: 7.7 us -> 3.78 us  [updated(): pl.pallas_call(update_kernel, name='update', out_shape=jax.ShapeDtypeStru...]
    all_to_all x1 -> x0, starting transfers between devices: 3.55 us -> none  [copies_to(): return lax.all_to_all(sent, axes, 0, 0, tiled=True)]
    ppermute x1, starting transfers between devices: 3.05 us -> 4.12 us  [per_device(): partner_grads = lax.ppermute(core_grads, CORE, SWAP)]
    pallas_call x1, Pallas kernels: 2.49 us -> 1.48 us  [started(): pl.pallas_call(start_kernel, name='start', out_shape=[jax.ShapeDtypeStruc...]
  transfers between devices with their start and end apart: 4 -> 7, of which waited for: 2 -> 2; matrix products, arithmetic and copies ran while one was open for 5% -> 5% of each run, Pallas kernels for 8% -> 4%
where the time goes in v2:
time: 97.3 us; the launch traced here: 97.1 us
  blocking collectives  62.2 us (64%)
  starting transfers between devices  12.9 us (13%)
  matrix products  9.01 us (9%)
  Pallas kernels  5.46 us (6%)
  waiting for transfers between devices  5.08 us (5%)
  other arithmetic  1.57 us (2%)
    all_to_all x3, blocking collectives, copies_to(): return lax.all_to_all(sent, axes, 0, 0, tiled=True)  62.2 us
    dot_general x5, matrix products, matmul(): return lax.dot_general(a, b, (over, ((), ())), preferred_element_type=f32)  5.27 us
    ppermute x1, waiting for transfers between devices, per_device(): far = lax.ppermute(near, 'zh', SWAP)  4.19 us
    ppermute x1, starting transfers between devices, per_device(): partner_grads = lax.ppermute(core_grads, CORE, SWAP)  4.12 us
    pallas_call x1, Pallas kernels, updated(): pl.pallas_call(update_kernel, name='update', out_shape=jax.ShapeDtypeStru...  3.78 us
    ppermute x3, starting transfers between devices, per_device(): lax.ppermute(near, 'zl', tuple(((i, (i + k) % count) for i in range(count...  3.44 us
    ppermute x1, starting transfers between devices, per_device(): far = lax.ppermute(near, 'zh', SWAP)  2.74 us
    ppermute x1, starting transfers between devices, per_device(): partner = lax.ppermute(mine, CORE, SWAP)  2.54 us
  transfers between devices with their start and end apart: 7, of which 2 were waited for; matrix products, arithmetic and copies ran while one was open for 5% of the time, Pallas kernels for 4%

profile of v2, /device:TPU:1, one launch (start us, length us, event | category | flops | bytes accessed | tf_op | source)
XLA Modules:
  0.0 97.1 jit_solution(6650879801481808297)
XLA Ops:
  0.7 0.0 copy-start
  0.7 1.5 %start.1 = (bf16[128,2,896]{2,1,0:T(2,128)(2,1)S(1)}, bf16[768,768]{1,0:T(8,128)(2,1)S(1)}) custom-call(bf16[2,768]{1,0:T(2,128)(2,1)} %features_ref.1, s32[2,8]{1,0:T(2,128)} %ids_ref.1, bf16[768,768]{1,0:T(8,128)(2,1)} %w_ref.2), custom_call_target="tpu_custom_call" | custom-call | bytes 2359296 | tf_op jit(solution)/shard_map/start/pallas_call | solution.py:66
  2.2 34.0 %all_to_all.15.tiles_ref = bf16[128,2,896]{2,1,0:T(2,128)(2,1)S(1)} all-to-all(bf16[128,2,896]{2,1,0:T(2,128)(2,1)S(1)} %get-tuple-element.32), channel_id=1, replica_groups=mesh['zl'=4,'core'=2,'zh'=2,'y'=4,'x'=4] {'y','x','zh','zl'}, dimensions={0} | all-to-all | bytes 917504 | tf_op jit(solution)/shard_map/all_to_all | solution.py:25
  36.2 0.1 rows.1
  36.3 2.5 %collective-permute-start = (bf16[256,896]{1,0:T(8,128)(2,1)S(1)}, bf16[256,896]{1,0:T(8,128)(2,1)S(1)}, u32[]{:S(2)}, u32[]{:S(2)}) collective-permute-start(bf16[256,896]{1,0:T(8,128)(2,1)S(1)} %rows.1), channel_id=1, source_target_pairs={{0,32},{32,0},{1,33},{33,1},{2,34},{34,2},{3,35},{35,3},{4,36},{36... | collective-permute-start | bytes 1376264 | tf_op jit(solution)/shard_map/ppermute | solution.py:227
  38.8 0.5 convolution_convert_fusion.1.ea_ref
  39.3 0.1 multiply_reduce_fusion.1
  39.4 0.0 copy-done
  39.5 1.6 %fusion.11.ga_ref = bf16[256,3072]{1,0:T(8,128)(2,1)S(1)} fusion(bf16[256,768]{1,0:T(8,128)(2,1)S(1)} %convolution_convert_fusion.1.ea_ref, bf16[3072,768]{1,0:T(8,128)(2,1)S(1)} %copy-done, s32[256]{0:T(256)S(1)} %convert_subtract_fusion.1), kind=kOutput, calls=%fused_computation.13 | convolution fusion | flops 1214251008 | bytes 6685696 | tf_op jit(solution)/shard_map/dot_general | solution.py:29
  41.1 0.0 collective-permute-done
  41.1 0.5 convolution_convert_fusion.eb_ref
  41.6 0.1 multiply_reduce_fusion
  41.7 1.6 %fusion.7.gb_ref = bf16[256,3072]{1,0:T(8,128)(2,1)S(1)} fusion(bf16[256,768]{1,0:T(8,128)(2,1)S(1)} %convolution_convert_fusion.eb_ref, bf16[3072,768]{1,0:T(8,128)(2,1)S(1)} %copy-done, s32[256]{0:T(256)S(1)} %convert_subtract_fusion), kind=kOutput, calls=%fused_computation.9 | convolution fusion | flops 1214251008 | bytes 6685696 | tf_op jit(solution)/shard_map/dot_general | solution.py:29
  43.3 1.4 %fusion.21 = f32[256,768]{1,0:T(8,128)S(1)} fusion(bf16[256,3072]{1,0:T(8,128)(2,1)S(1)} %fusion.7.gb_ref, bf16[3072,768]{1,0:T(8,128)(2,1)S(1)} %copy-done), kind=kOutput, calls=%fused_computation.36 | convolution fusion | flops 1207959552 | bytes 7077888 | tf_op jit(solution)/shard_map/dot_general | solution.py:240
  44.7 0.1 collective-permute-start.1
  44.8 1.4 %fusion.20 = f32[256,768]{1,0:T(8,128)S(1)} fusion(bf16[256,3072]{1,0:T(8,128)(2,1)S(1)} %fusion.11.ga_ref, bf16[3072,768]{1,0:T(8,128)(2,1)S(1)} %copy-done), kind=kOutput, calls=%fused_computation.35 | convolution fusion | flops 1207959552 | bytes 7077888 | tf_op jit(solution)/shard_map/dot_general | solution.py:242
  46.2 0.9 collective-permute-done.1
  47.1 0.1 add.43
  47.2 16.7 %all_to_all.16.pieces_ref = f32[16,16,768]{2,1,0:T(8,128)S(1)} all-to-all(f32[16,16,768]{2,1,0:T(8,128)S(1)} %bitcast.21), channel_id=1, replica_groups=mesh['zl'=4,'core'=2,'zh'=2,'y'=4,'x'=4] {'y','x'}, dimensions={0} | all-to-all | bytes 1572864 | tf_op jit(solution)/shard_map/all_to_all | solution.py:25
  64.0 0.2 collective-permute-start.2
  64.1 0.5 collective-permute-start.3
  64.6 2.8 %collective-permute-start.4 = (f32[16,768]{1,0:T(8,128)S(1)}, f32[16,768]{1,0:T(8,128)S(1)}, u32[]{:S(2)}, u32[]{:S(2)}) collective-permute-start(f32[16,768]{1,0:T(8,128)S(1)} %bitcast.19), channel_id=1, source_target_pairs={{0,192},{64,0},{128,64},{192,128},{1,193},{65,1},{129,65},{193,129... | collective-permute-start | bytes 147464 | tf_op jit(solution)/shard_map/ppermute | solution.py:251
  67.4 3.8 %update.1 = bf16[3072,768]{1,0:T(8,128)(2,1)} custom-call(bf16[256,3072]{1,0:T(8,128)(2,1)S(1)} %fusion.11.ga_ref, bf16[256,3072]{1,0:T(8,128)(2,1)S(1)} %fusion.7.gb_ref, bf16[256,768]{1,0:T(8,128)(2,1)S(1)} %convolution_convert_fusion.1.ea_ref, bf16[256,768]{1,0:T(8,128)(2,1)S(1)} %convolution_convert_fusion.eb_ref, bf16[3072,768]{1,0:T(8,128)(2,1)S(1)} %copy-done), custom_call_target="tpu_custom_call" | custom-call | flops 2415919104 | bytes 4718592 | tf_op jit(solution)/shard_map/update/pallas_call | solution.py:196
  71.2 0.0 collective-permute-done.2.refs_2_
  71.2 0.0 collective-permute-done.3.refs_3_
  71.2 0.0 collective-permute-done.4.refs_4_
  71.3 2.7 %collective-permute-start.5 = (f32[16,768]{1,0:T(8,128)S(1)}, f32[16,768]{1,0:T(8,128)S(1)}, u32[]{:S(2)}, u32[]{:S(2)}) collective-permute-start(f32[16,768]{1,0:T(8,128)S(1)} %line_sum.1.near_ref), channel_id=1, source_target_pairs={{0,16},{16,0},{1,17},{17,1},{2,18},{18,2},{3,19},{19,3},{4,20},{20... | collective-permute-start | bytes 147464 | tf_op jit(solution)/shard_map/ppermute | solution.py:256
  74.0 4.2 %collective-permute-done.5.far_ref = f32[16,768]{1,0:T(8,128)S(1)} collective-permute-done((f32[16,768]{1,0:T(8,128)S(1)}, f32[16,768]{1,0:T(8,128)S(1)}, u32[]{:S(2)}, u32[]{:S(2)}) %collective-permute-start.5) | collective-permute-done | bytes 49184 | tf_op jit(solution)/shard_map/ppermute | solution.py:256
  78.3 11.4 %all_to_all.17 = bf16[16,16,768]{2,1,0:T(8,128)(2,1)S(1)} all-to-all(bf16[16,16,768]{2,1,0:T(8,128)(2,1)S(1)} %get-tuple-element.50), channel_id=1, replica_groups=mesh['zl'=4,'core'=2,'zh'=2,'y'=4,'x'=4] {'y','x'}, dimensions={0} | all-to-all | bytes 786432 | tf_op jit(solution)/shard_map/all_to_all | solution.py:25
  89.7 4.1 %collective-permute-start.6 = (bf16[256,768]{1,0:T(8,128)(2,1)S(1)}, bf16[256,768]{1,0:T(8,128)(2,1)S(1)}, u32[]{:S(2)}, u32[]{:S(2)}) collective-permute-start(bf16[256,768]{1,0:T(8,128)(2,1)S(1)} %bitcast.22), channel_id=1, source_target_pairs={{0,32},{32,0},{1,33},{33,1},{2,34},{34,2},{3,35},{35,3},{4,36},{36... | collective-permute-start | bytes 1179656 | tf_op jit(solution)/shard_map/ppermute | solution.py:262
  93.8 1.0 %convolution_convert_fusion.2 = bf16[2,768]{1,0:T(2,128)(2,1)} fusion(bf16[768,768]{1,0:T(8,128)(2,1)S(1)} %get-tuple-element.33, bf16[16,768]{1,0:T(8,128)(2,1)S(1)} %get-tuple-element.52, u32[]{:T(128)S(6)} %convert_element_type.47), kind=kOutput, calls=%fused_computation.19 | convolution fusion | flops 2360832 | bytes 1185796 | tf_op jit(solution)/shard_map/dot_general | solution.py:29
  94.8 0.5 fusion.12
  95.4 0.0 collective-permute-done.6
  95.4 0.5 fusion.15
  95.9 1.2 %add_convert_fusion = bf16[768,768]{1,0:T(8,128)(2,1)} fusion(f32[768,768]{1,0:T(8,128)S(1)} %fusion.12, f32[768,768]{1,0:T(8,128)S(1)} %fusion.15), kind=kLoop, calls=%fused_computation.16 | loop fusion | flops 1179648 | bytes 5898240 | tf_op jit(solution)/shard_map/convert_element_type | solution.py:265
  (6 shorter events, 0.1 us)
Async XLA Ops:
  0.7 38.8 %copy-start = (bf16[3072,768]{1,0:T(8,128)(2,1)S(1)}, bf16[3072,768]{1,0:T(8,128)(2,1)}, u32[]{:S(2)}) copy-start(bf16[3072,768]{1,0:T(8,128)(2,1)} %w_ref.3) | copy-start | bytes 14155780
  36.3 4.8 %collective-permute-start = (bf16[256,896]{1,0:T(8,128)(2,1)S(1)}, bf16[256,896]{1,0:T(8,128)(2,1)S(1)}, u32[]{:S(2)}, u32[]{:S(2)}) collective-permute-start(bf16[256,896]{1,0:T(8,128)(2,1)S(1)} %rows.1), channel_id=1, source_target_pairs={{0,32},{32,0},{1,33},{33,1},{2,34},{34,2},{3,35},{35,3},{4,36},{36... | collective-permute-start | bytes 1376264 | tf_op jit(solution)/shard_map/ppermute | solution.py:227
  44.7 2.4 %collective-permute-start.1 = (f32[256,768]{1,0:T(8,128)S(1)}, f32[256,768]{1,0:T(8,128)S(1)}, u32[]{:S(2)}, u32[]{:S(2)}) collective-permute-start(f32[256,768]{1,0:T(8,128)S(1)} %fusion.21), channel_id=1, source_target_pairs={{0,32},{32,0},{1,33},{33,1},{2,34},{34,2},{3,35},{35,3},{4,36},{36... | collective-permute-start | bytes 2359304 | tf_op jit(solution)/shard_map/ppermute | solution.py:241
  64.0 7.2 %collective-permute-start.2 = (f32[16,768]{1,0:T(8,128)S(1)}, f32[16,768]{1,0:T(8,128)S(1)}, u32[]{:S(2)}, u32[]{:S(2)}) collective-permute-start(f32[16,768]{1,0:T(8,128)S(1)} %bitcast.17), channel_id=1, source_target_pairs={{0,128},{64,192},{128,0},{192,64},{1,129},{65,193},{129,1},{193,65... | collective-permute-start | bytes 147464 | tf_op jit(solution)/shard_map/ppermute | solution.py:251
  64.1 7.1 %collective-permute-start.3 = (f32[16,768]{1,0:T(8,128)S(1)}, f32[16,768]{1,0:T(8,128)S(1)}, u32[]{:S(2)}, u32[]{:S(2)}) collective-permute-start(f32[16,768]{1,0:T(8,128)S(1)} %bitcast.18), channel_id=1, source_target_pairs={{0,64},{64,128},{128,192},{192,0},{1,65},{65,129},{129,193},{193,1... | collective-permute-start | bytes 147464 | tf_op jit(solution)/shard_map/ppermute | solution.py:251
  64.6 6.6 %collective-permute-start.4 = (f32[16,768]{1,0:T(8,128)S(1)}, f32[16,768]{1,0:T(8,128)S(1)}, u32[]{:S(2)}, u32[]{:S(2)}) collective-permute-start(f32[16,768]{1,0:T(8,128)S(1)} %bitcast.19), channel_id=1, source_target_pairs={{0,192},{64,0},{128,64},{192,128},{1,193},{65,1},{129,65},{193,129... | collective-permute-start | bytes 147464 | tf_op jit(solution)/shard_map/ppermute | solution.py:251
  71.3 6.9 %collective-permute-start.5 = (f32[16,768]{1,0:T(8,128)S(1)}, f32[16,768]{1,0:T(8,128)S(1)}, u32[]{:S(2)}, u32[]{:S(2)}) collective-permute-start(f32[16,768]{1,0:T(8,128)S(1)} %line_sum.1.near_ref), channel_id=1, source_target_pairs={{0,16},{16,0},{1,17},{17,1},{2,18},{18,2},{3,19},{19,3},{4,20},{20... | collective-permute-start | bytes 147464 | tf_op jit(solution)/shard_map/ppermute | solution.py:256
  89.7 5.7 %collective-permute-start.6 = (bf16[256,768]{1,0:T(8,128)(2,1)S(1)}, bf16[256,768]{1,0:T(8,128)(2,1)S(1)}, u32[]{:S(2)}, u32[]{:S(2)}) collective-permute-start(bf16[256,768]{1,0:T(8,128)(2,1)S(1)} %bitcast.22), channel_id=1, source_target_pairs={{0,32},{32,0},{1,33},{33,1},{2,34},{34,2},{3,35},{35,3},{4,36},{36... | collective-permute-start | bytes 1179656 | tf_op jit(solution)/shard_map/ppermute | solution.py:262
